TPU v7x, 32 devices: a whole 2x2x4 slice. The times are simulated.
32 devices in a mesh: cuts: 2 (over x), mode: 8 (over z, y), branch: 2 (over core).
Axes of the slice: x: 2, y: 2, z: 4, core: 2. Of those that a mesh axis runs over, the one named last changes fastest.
Arguments:
- leaves: bfloat16 [8, 2, 32, 512, 512], P('branch', None, ('cuts', 'mode')), parts along dimension 2, may hold values from -0.1875 to 0.1875
- join_order: int32 [7], replicated, may hold values from 0 to 1
- slice_values: int32 [32], P(('cuts', 'mode')), parts along dimension 0, may hold values from 0 to 1
- boundary: bfloat16 [2, 2, 512, 512], replicated, may hold values from -4 to 4
Outputs:
- amplitudes: float32 [2, 32, 512, 512], P(None, ('cuts', 'mode'), 'branch'), parts along dimension 1
There are 2 independent parts, one for each index of `cuts`. A program takes and returns all parts, laid end to end along the dimension named above; an argument that names none is the same for every part. Nothing has to cross between parts.
Inputs may be any that keep to these rules, and one draw needn't show every extreme that they name: `join_order`: 1 puts the second operand of the join on the left.
All inputs are finite; a program needn't handle non-finite values.
Results may differ from a plain program's by a relative error of at most 0.0076.
Values may be sent and summed in bfloat16 or wider, within the bound.
A program may use at most 64 MiB of HBM per device.

v0:
```python
import jax
import jax.numpy as jnp
from jax import lax
from jax.sharding import PartitionSpec as P


def from_partner(value, axis, bit):
    mask = 2**bit
    pairs = [(source, source ^ mask) for source in range(lax.axis_size(axis))]
    return lax.ppermute(value, axis, pairs)


def complex_sums(left_op, right_op):
    spec = "bij,bjk->bik"
    real_part = jnp.einsum(
        spec, left_op[0], right_op[0], preferred_element_type=jnp.float32
    ) - jnp.einsum(spec, left_op[1], right_op[1], preferred_element_type=jnp.float32)
    imag_part = jnp.einsum(
        spec, left_op[0], right_op[1], preferred_element_type=jnp.float32
    ) + jnp.einsum(spec, left_op[1], right_op[0], preferred_element_type=jnp.float32)
    return jnp.stack([real_part, imag_part])


def complex_product(left_op, right_op):
    return complex_sums(left_op, right_op).astype(jnp.bfloat16)


def join_pair(left_op, right_op, swapped):
    return lax.cond(
        swapped == 1,
        lambda: complex_product(right_op, left_op),
        lambda: complex_product(left_op, right_op),
    )


def split_rows(tensor, blocks):
    shape = tensor.shape
    return tensor.reshape(shape[0], shape[1], blocks, shape[2] // blocks, shape[3])


def merge_rows(tensor):
    shape = tensor.shape
    width = shape[4]
    total_rows = shape[1] * shape[2] * shape[3]
    return tensor.reshape(shape[0], total_rows // width, width, width)


def per_device(leaves, join_order, slice_values, boundary):
    blocks = lax.axis_size("mode")
    branch_index = lax.axis_index("branch")
    base_index = 2 * branch_index
    first_pair = join_pair(leaves[0], leaves[1], join_order[base_index])
    second_pair = join_pair(leaves[2], leaves[3], join_order[base_index + 1])
    first_pair, second_pair = (
        lax.all_to_all(
            split_rows(first_pair, blocks), "mode", split_axis=2, concat_axis=1, tiled=True
        ),
        lax.all_to_all(
            split_rows(second_pair, blocks), "mode", split_axis=2, concat_axis=1, tiled=True
        ),
    )
    first_pair = merge_rows(first_pair)
    second_pair = merge_rows(second_pair)
    middle = join_pair(first_pair, second_pair, join_order[4 + branch_index])
    middle = merge_rows(
        lax.all_to_all(split_rows(middle, blocks), "mode", split_axis=2, concat_axis=1, tiled=True)
    )
    width = middle.shape[3]
    half_rows = width // 2
    chosen = jnp.where(
        slice_values[None, :, None, None] == 1, boundary[1][:, None], boundary[0][:, None]
    )
    top_order = join_order[-1]
    partner = from_partner(middle, "branch", 0)
    is_first = branch_index == 0
    upper = jnp.where(is_first, middle, partner)
    lower = jnp.where(is_first, partner, middle)
    leading = jnp.where(top_order == 1, lower, upper)
    trailing = jnp.where(top_order == 1, upper, lower)
    leading = lax.dynamic_slice_in_dim(leading, branch_index * half_rows, half_rows, 2)
    top_half = complex_product(leading, trailing)
    amplitudes = complex_sums(top_half, chosen)
    return amplitudes


def solution(mesh):
    in_specs = (P("branch", None, ("cuts", "mode"), None, None), P(), P(("cuts", "mode")), P())
    out_specs = P(None, ("cuts", "mode"), "branch", None)
    return jax.shard_map(
        per_device, mesh=mesh, in_specs=in_specs, out_specs=out_specs, check_vma=False
    )
```

profile of v0, /device:TPU:0, one launch (start us, length us, event | category | flops | bytes accessed | tf_op | source)
XLA Modules:
  0.0 195.7 jit_solution(156778789101351986)
XLA Ops:
  0.0 5.7 %slice_bitcast_fusion = (bf16[2,2,512,512]{3,2,1,0:T(8,128)(2,1)}, bf16[2,2,512,512]{3,2,1,0:T(8,128)(2,1)S(1)}, bf16[2,2,512,512]{3,2,1,0:T(8,128)(2,1)}, bf16[2,2,512,512]{3,2,1,0:T(8,128)(2,1)}) fusion(bf16[4,2,2,512,512]{4,3,2,1,0:T(8,128)(2,1)} %param.10), kind=kLoop, calls=%fused_computation.127 | loop fusion | bytes 16777216 | tf_op jit(solution)/shard_map/squeeze | solution.py:53
  7.0 6.6 %conditional.7 = (bf16[2,2,512,512]{3,2,1,0:T(8,128)(2,1)}) conditional(s32[]{:T(128)} %bitcast.45, (bf16[2,2,512,512]{3,2,1,0:T(8,128)(2,1)}, bf16[2,2,512,512]{3,2,1,0:T(8,128)(2,1)}) %tuple.34, (bf16[2,2,512,512]{3,2,1,0:T(8,128)(2,1)}, bf16[2,2,512,512]{3,2,1,0:T(8,128)(2,1)}) %tuple.35), branch_computations={%region_2.0_spmd, %region_3.0_spmd} | conditional | flops 2150629376 | bytes 39845952
  7.1 2.4 %fusion.36 = f32[2,512,512]{2,1,0:T(8,128)S(1)} fusion(bf16[2,2,512,512]{3,2,1,0:T(8,128)(2,1)} %get-tuple-element.49, bf16[2,2,512,512]{3,2,1,0:T(8,128)(2,1)} %get-tuple-element.48), kind=kOutput, calls=%fused_computation.45 | convolution fusion | flops 536870912 | bytes 4194304 | tf_op jit(solution)/shard_map/cond/branch_0_fun/bij,bjk->bik/dot_general | solution.py:18
  11.3 0.7 subtract_bitcast_fusion.2
  12.1 1.6 pad_maximum_fusion.2
  13.6 3.2 %copy.11 = bf16[2,2,8,64,512]{4,3,1,0,2:T(8,128)(2,1)} copy(bf16[2,2,8,64,512]{4,3,2,1,0:T(8,128)(2,1)} %bitcast.213) | data formatting | bytes 4194304 | tf_op jit(solution)/shard_map/reshape | solution.py:38
  16.8 7.3 %all-to-all-start.1 = ((bf16[2,2,8,64,512]{4,3,1,0,2:T(8,128)(2,1)}), bf16[2,2,8,64,512]{4,3,1,0,2:T(8,128)(2,1)}, u32[]{:S(2)}, u32[]{:S(2)}) async-start(bf16[2,2,8,64,512]{4,3,1,0,2:T(8,128)(2,1)} %copy.11), calls=%async_computation.1 | async-start | bytes 4194304 | tf_op jit(solution)/shard_map/all_to_all | solution.py:58
  24.7 4.5 %conditional.6 = (bf16[2,2,512,512]{3,2,1,0:T(8,128)(2,1)S(1)}) conditional(s32[]{:T(128)} %bitcast.38, (bf16[2,2,512,512]{3,2,1,0:T(8,128)(2,1)}, bf16[2,2,512,512]{3,2,1,0:T(8,128)(2,1)S(1)}) %tuple.32, (bf16[2,2,512,512]{3,2,1,0:T(8,128)(2,1)S(1)}, bf16[2,2,512,512]{3,2,1,0:T(8,128)(2,1)}) %tuple.33), branch_computations={%region_0.0_spmd, %region_1.0_spmd} | conditional | flops 2150629376 | bytes 31457316
  24.8 2.1 %fusion.18 = f32[2,512,512]{2,1,0:T(8,128)S(1)} fusion(bf16[2,2,512,512]{3,2,1,0:T(8,128)(2,1)} %get-tuple-element.47, bf16[2,2,512,512]{3,2,1,0:T(8,128)(2,1)S(1)} %get-tuple-element.46), kind=kOutput, calls=%fused_computation.24 | convolution fusion | flops 536870912 | bytes 4194304 | tf_op jit(solution)/shard_map/cond/branch_1_fun/bij,bjk->bik/dot_general | solution.py:18
  28.3 0.7 subtract_bitcast_fusion.1
  29.2 1.5 copy.9
  30.7 41.7 %all-to-all-done.1 = bf16[2,2,8,64,512]{4,3,1,0,2:T(8,128)(2,1)} async-done(((bf16[2,2,8,64,512]{4,3,1,0,2:T(8,128)(2,1)}), bf16[2,2,8,64,512]{4,3,1,0,2:T(8,128)(2,1)}, u32[]{:S(2)}, u32[]{:S(2)}) %all-to-all-start.1) | async-done | bytes 2097184 | tf_op jit(solution)/shard_map/all_to_all | solution.py:58
  72.4 4.4 %all-to-all-start = ((bf16[2,2,8,64,512]{4,3,1,0,2:T(8,128)(2,1)}), bf16[2,2,8,64,512]{4,3,1,0,2:T(8,128)(2,1)}, u32[]{:S(2)}, u32[]{:S(2)}) async-start(bf16[2,2,8,64,512]{4,3,1,0,2:T(8,128)(2,1)} %copy.9), calls=%async_computation | async-start | bytes 4194304 | tf_op jit(solution)/shard_map/all_to_all | solution.py:55
  77.5 1.8 copy.12
  79.3 45.3 %all-to-all-done = bf16[2,2,8,64,512]{4,3,1,0,2:T(8,128)(2,1)} async-done(((bf16[2,2,8,64,512]{4,3,1,0,2:T(8,128)(2,1)}), bf16[2,2,8,64,512]{4,3,1,0,2:T(8,128)(2,1)}, u32[]{:S(2)}, u32[]{:S(2)}) %all-to-all-start) | async-done | bytes 2097184 | tf_op jit(solution)/shard_map/all_to_all | solution.py:55
  124.6 1.8 copy.10
  126.4 3.3 %conditional.8 = (bf16[2,2,512,512]{3,2,1,0:T(8,128)(2,1)S(1)}) conditional(s32[]{:T(128)} %bitcast.37, (bf16[2,2,512,512]{3,2,1,0:T(8,128)(2,1)S(1)}, bf16[2,2,512,512]{3,2,1,0:T(8,128)(2,1)S(1)}) %tuple.55, (bf16[2,2,512,512]{3,2,1,0:T(8,128)(2,1)S(1)}, bf16[2,2,512,512]{3,2,1,0:T(8,128)(2,1)S(1)}) %tuple.56), branch_computations={%region_4.0_spmd, %region_5.0_spmd} | conditional | flops 2150629376 | bytes 23068680
  127.2 0.7 add_bitcast_fusion.4
  129.9 51.8 %all_to_all.45 = bf16[2,2,8,64,512]{4,3,1,0,2:T(8,128)(2,1)S(1)} all-to-all(bf16[2,2,8,64,512]{4,3,1,0,2:T(8,128)(2,1)S(1)} %copy.13), channel_id=1, replica_groups=mesh['cuts'=2,'mode'=8,'branch'=2] {'mode'}, dimensions={2} | all-to-all | bytes 4194304 | tf_op jit(solution)/shard_map/all_to_all | solution.py:66
  181.7 1.5 copy.14
  183.9 1.7 slice_bitcast_fusion.9
  185.9 1.9 collective-permute-done
  187.8 2.6 %broadcast_select_fusion.3 = (bf16[2,2,512,512]{3,2,1,0:T(8,128)(2,1)S(1)}, bf16[2,2,512,512]{3,2,1,0:T(8,128)(2,1)S(1)}, bf16[2,2,512,512]{3,2,1,0:T(8,128)(2,1)S(1)}) fusion(pred[]{:T(512)} %bitcast.36, bf16[2,2,512,512]{3,2,1,0:T(8,128)(2,1)} %collective-permute-done, bf16[2,2,512,512]{3,2,1,0:T(8,128)(2,1)} %bitcast.59, pred[]{:T(512)S(6)} %eq.28), kind=kLoop, calls=%fused_computation.134 | loop fusion | flops 3145728 | bytes 10485762 | tf_op jit(solution)/shard_map/jit(_where)/select_n | solution.py:79
  194.2 1.5 pad_maximum_fusion.6
  (33 shorter events, 10.7 us)
Async XLA Ops:
  0.0 5.7 %copy-start.6 = (s32[7]{0:T(128)S(1)}, s32[7]{0:T(128)}, u32[]{:S(2)}) copy-start(s32[7]{0:T(128)} %param.11) | copy-start | bytes 88
  7.0 2.4 %copy-start.2 = (bf16[2,2,512,512]{3,2,1,0:T(8,128)(2,1)S(1)}, bf16[2,2,512,512]{3,2,1,0:T(8,128)(2,1)}, u32[]{:S(2)}) copy-start(bf16[2,2,512,512]{3,2,1,0:T(8,128)(2,1)} %get-tuple-element.49) | copy-start | bytes 6291460 | tf_op jit(solution)/shard_map/conditional.1
  7.1 2.8 %copy-start.4 = (bf16[2,2,512,512]{3,2,1,0:T(8,128)(2,1)S(1)}, bf16[2,2,512,512]{3,2,1,0:T(8,128)(2,1)}, u32[]{:S(2)}) copy-start(bf16[2,2,512,512]{3,2,1,0:T(8,128)(2,1)} %get-tuple-element.48) | copy-start | bytes 6291460 | tf_op jit(solution)/shard_map/conditional.1
  16.8 55.7 %all-to-all-start.1 = ((bf16[2,2,8,64,512]{4,3,1,0,2:T(8,128)(2,1)}), bf16[2,2,8,64,512]{4,3,1,0,2:T(8,128)(2,1)}, u32[]{:S(2)}, u32[]{:S(2)}) async-start(bf16[2,2,8,64,512]{4,3,1,0,2:T(8,128)(2,1)} %copy.11), calls=%async_computation.1 | async-start | bytes 4194304 | tf_op jit(solution)/shard_map/all_to_all | solution.py:58
  24.8 2.1 %copy-start.1 = (bf16[2,2,512,512]{3,2,1,0:T(8,128)(2,1)S(1)}, bf16[2,2,512,512]{3,2,1,0:T(8,128)(2,1)}, u32[]{:S(2)}) copy-start(bf16[2,2,512,512]{3,2,1,0:T(8,128)(2,1)} %get-tuple-element.47) | copy-start | bytes 6291460 | tf_op jit(solution)/shard_map/conditional
  72.4 52.2 %all-to-all-start = ((bf16[2,2,8,64,512]{4,3,1,0,2:T(8,128)(2,1)}), bf16[2,2,8,64,512]{4,3,1,0,2:T(8,128)(2,1)}, u32[]{:S(2)}, u32[]{:S(2)}) async-start(bf16[2,2,8,64,512]{4,3,1,0,2:T(8,128)(2,1)} %copy.9), calls=%async_computation | async-start | bytes 4194304 | tf_op jit(solution)/shard_map/all_to_all | solution.py:55
  181.7 2.2 %copy-start.7 = (s32[2]{0:T(128)S(1)}, s32[2]{0:T(128)}, u32[]{:S(2)}) copy-start(s32[2]{0:T(128)} %param.12) | copy-start | bytes 28
  183.3 4.5 %collective-permute-start = (bf16[2,2,512,512]{3,2,1,0:T(8,128)(2,1)}, bf16[2,2,512,512]{3,2,1,0:T(8,128)(2,1)}, u32[]{:S(2)}, u32[]{:S(2)}) collective-permute-start(bf16[2,2,512,512]{3,2,1,0:T(8,128)(2,1)} %bitcast.59), channel_id=1, source_target_pairs={{0,1},{1,0},{2,3},{3,2},{4,5},{5,4},{6,7},{7,6},{8,9},{9,8},{10,11... | collective-permute-start | bytes 6291464 | tf_op jit(solution)/shard_map/ppermute | solution.py:10
where the time goes:
time: 196 us
  waiting for transfers between devices  88.9 us (45%)
  blocking collectives  51.8 us (26%)
  local copies, waits for them, and re-layouts  18.6 us (9%)
  matrix products  15.1 us (8%)
  starting transfers between devices  11.7 us (6%)
  other arithmetic  6.63 us (3%)
  between operations  2.74 us (1%)
    all_to_all x1, blocking collectives, per_device(): lax.all_to_all(split_rows(middle, blocks), 'mode', split_axis=2, concat_a...  51.8 us
    all_to_all x1, waiting for transfers between devices, per_device(): lax.all_to_all(split_rows(first_pair, blocks), 'mode', split_axis=2, conc...  45.3 us
    all_to_all x1, waiting for transfers between devices, per_device(): lax.all_to_all(split_rows(second_pair, blocks), 'mode', split_axis=2, con...  41.7 us
    all_to_all x1, starting transfers between devices, per_device(): lax.all_to_all(split_rows(second_pair, blocks), 'mode', split_axis=2, con...  7.31 us
    dot_general x5, matrix products, complex_sums(): jnp.einsum(spec, left_op[0], right_op[1], preferred_element_type=jnp.floa...  6.06 us
    squeeze x1, local copies, waits for them, and re-layouts, per_device(): second_pair = join_pair(leaves[2], leaves[3], join_order[base_index + 1])  5.73 us
    reshape x3, local copies, waits for them, and re-layouts, split_rows(): tensor.reshape(shape[0], shape[1], blocks, shape[2] // blocks, shape[3])  4.91 us
    all_to_all x1, starting transfers between devices, per_device(): lax.all_to_all(split_rows(first_pair, blocks), 'mode', split_axis=2, conc...  4.35 us
  transfers between devices with their start and end apart: 3, of which 3 were waited for; matrix products, arithmetic and copies ran while one was open for 5% of the time, Pallas kernels for 0%

commit v1 on v0

--- a/solution.py
+++ b/solution.py
@@ -55,8 +55,16 @@
         lax.all_to_all(
             split_rows(first_pair, blocks), "mode", split_axis=2, concat_axis=1, tiled=True
         ),
-        lax.all_to_all(
-            split_rows(second_pair, blocks), "mode", split_axis=2, concat_axis=1, tiled=True
+        jnp.concatenate(
+            lax.all_to_all(
+                jnp.stack(
+                    jnp.split(split_rows(second_pair, blocks), lax.axis_size("mode"), axis=2)
+                ),
+                "mode",
+                0,
+                0,
+            ),
+            axis=1,
         ),
     )
     first_pair = merge_rows(first_pair)

time: 196 us -> 204 us (1.041)
  local copies, waits for them, and re-layouts: 18.6 us -> 27.4 us
    unnamed x4 -> x11, local copies, waits for them, and re-layouts: 0.01 us -> 11.7 us
    reshape x3 -> x2, local copies, waits for them, and re-layouts: 4.91 us -> 1.7 us  [split_rows(): tensor.reshape(shape[0], shape[1], blocks, shape[2] // blocks, shape[3])]
where the time goes in v1:
time: 204 us
  waiting for transfers between devices  88.8 us (44%)
  blocking collectives  51.8 us (25%)
  local copies, waits for them, and re-layouts  27.4 us (13%)
  matrix products  15.1 us (7%)
  starting transfers between devices  11.7 us (6%)
  other arithmetic  5.93 us (3%)
  between operations  2.75 us (1%)
    all_to_all x1, blocking collectives, per_device(): lax.all_to_all(split_rows(middle, blocks), 'mode', split_axis=2, concat_a...  51.8 us
    all_to_all x1, waiting for transfers between devices, per_device(): lax.all_to_all(split_rows(first_pair, blocks), 'mode', split_axis=2, conc...  45.4 us
    all_to_all x1, waiting for transfers between devices, per_device(): lax.all_to_all(jnp.stack(jnp.split(split_rows(second_pair, blocks), lax.a...  41.8 us
    unnamed x11, local copies, waits for them, and re-layouts  11.7 us
    all_to_all x1, starting transfers between devices, per_device(): lax.all_to_all(jnp.stack(jnp.split(split_rows(second_pair, blocks), lax.a...  7.31 us
    squeeze x1, local copies, waits for them, and re-layouts, per_device(): second_pair = join_pair(leaves[2], leaves[3], join_order[base_index + 1])  5.7 us
    dot_general x5, matrix products, complex_sums(): jnp.einsum(spec, left_op[0], right_op[0], preferred_element_type=jnp.floa...  4.68 us
    dot_general x5, matrix products, complex_sums(): jnp.einsum(spec, left_op[0], right_op[1], preferred_element_type=jnp.floa...  4.37 us
  transfers between devices with their start and end apart: 3, of which 3 were waited for; matrix products, arithmetic and copies ran while one was open for 5% of the time, Pallas kernels for 0%

profile of v1, /device:TPU:0, one launch (start us, length us, event | category | flops | bytes accessed | tf_op | source)
XLA Modules:
  0.0 203.8 jit_solution(6147217979707647763)
XLA Ops:
  0.0 5.7 %slice_bitcast_fusion = (bf16[2,2,512,512]{3,2,1,0:T(8,128)(2,1)}, bf16[2,2,512,512]{3,2,1,0:T(8,128)(2,1)S(1)}, bf16[2,2,512,512]{3,2,1,0:T(8,128)(2,1)}, bf16[2,2,512,512]{3,2,1,0:T(8,128)(2,1)}) fusion(bf16[4,2,2,512,512]{4,3,2,1,0:T(8,128)(2,1)} %param.10), kind=kLoop, calls=%fused_computation.127 | loop fusion | bytes 16777216 | tf_op jit(solution)/shard_map/squeeze | solution.py:53
  7.0 6.5 %conditional.12 = (bf16[2,2,8,64,512]{4,3,2,1,0:T(8,128)(2,1)}) conditional(s32[]{:T(128)} %bitcast.45, (bf16[2,2,512,512]{3,2,1,0:T(8,128)(2,1)}, bf16[2,2,512,512]{3,2,1,0:T(8,128)(2,1)}) %tuple.57, (bf16[2,2,512,512]{3,2,1,0:T(8,128)(2,1)}, bf16[2,2,512,512]{3,2,1,0:T(8,128)(2,1)}) %tuple.58), branch_computations={%region_2.0_spmd, %region_3.0_spmd} | conditional | flops 2150629376 | bytes 39845952 | solution.py:29
  7.0 2.4 %fusion.42 = f32[2,512,512]{2,1,0:T(8,128)S(1)} fusion(bf16[2,2,512,512]{3,2,1,0:T(8,128)(2,1)} %get-tuple-element.136, bf16[2,2,512,512]{3,2,1,0:T(8,128)(2,1)} %get-tuple-element.135), kind=kOutput, calls=%fused_computation.51 | convolution fusion | flops 536870912 | bytes 4194304 | tf_op jit(solution)/shard_map/cond/branch_0_fun/bij,bjk->bik/dot_general | solution.py:15
  13.5 1.7 fusion.123
  15.2 1.7 fusion.122
  16.9 1.7 fusion.121
  18.5 1.7 fusion.120
  20.2 1.7 fusion.119
  21.9 1.7 fusion.118
  23.6 1.7 fusion.117
  25.3 1.7 fusion.116
  26.9 7.3 %all-to-all-start.1 = ((bf16[8,2,2,1,64,512]{5,4,2,1,3,0:T(8,128)(2,1)}), bf16[8,2,2,1,64,512]{5,4,2,1,3,0:T(8,128)(2,1)}, u32[]{:S(2)}, u32[]{:S(2)}) async-start(bf16[8,2,2,1,64,512]{5,4,2,1,3,0:T(8,128)(2,1)} %fusion.116), calls=%async_computation.1 | async-start | bytes 4194304 | tf_op jit(solution)/shard_map/all_to_all | solution.py:59
  34.9 4.5 %conditional.5 = (bf16[2,2,512,512]{3,2,1,0:T(8,128)(2,1)S(1)}) conditional(s32[]{:T(128)} %bitcast.38, (bf16[2,2,512,512]{3,2,1,0:T(8,128)(2,1)}, bf16[2,2,512,512]{3,2,1,0:T(8,128)(2,1)S(1)}) %tuple.55, (bf16[2,2,512,512]{3,2,1,0:T(8,128)(2,1)S(1)}, bf16[2,2,512,512]{3,2,1,0:T(8,128)(2,1)}) %tuple.56), branch_computations={%region_0.0_spmd, %region_1.0_spmd} | conditional | flops 2150629376 | bytes 31457316
  34.9 2.1 %fusion.18 = f32[2,512,512]{2,1,0:T(8,128)S(1)} fusion(bf16[2,2,512,512]{3,2,1,0:T(8,128)(2,1)} %get-tuple-element.134, bf16[2,2,512,512]{3,2,1,0:T(8,128)(2,1)S(1)} %get-tuple-element.133), kind=kOutput, calls=%fused_computation.24 | convolution fusion | flops 536870912 | bytes 4194304 | tf_op jit(solution)/shard_map/cond/branch_1_fun/bij,bjk->bik/dot_general | solution.py:18
  40.8 41.8 %all-to-all-done.1 = bf16[8,2,2,1,64,512]{5,4,2,1,3,0:T(8,128)(2,1)} async-done(((bf16[8,2,2,1,64,512]{5,4,2,1,3,0:T(8,128)(2,1)}), bf16[8,2,2,1,64,512]{5,4,2,1,3,0:T(8,128)(2,1)}, u32[]{:S(2)}, u32[]{:S(2)}) %all-to-all-start.1) | async-done | bytes 2097184 | tf_op jit(solution)/shard_map/all_to_all | solution.py:59
  82.6 4.4 %all-to-all-start = ((bf16[2,2,8,64,512]{4,3,1,0,2:T(8,128)(2,1)}), bf16[2,2,8,64,512]{4,3,1,0,2:T(8,128)(2,1)}, u32[]{:S(2)}, u32[]{:S(2)}) async-start(bf16[2,2,8,64,512]{4,3,1,0,2:T(8,128)(2,1)} %copy.24), calls=%async_computation | async-start | bytes 4194304 | tf_op jit(solution)/shard_map/all_to_all | solution.py:55
  87.6 1.8 copy.33
  89.3 45.4 %all-to-all-done = bf16[2,2,8,64,512]{4,3,1,0,2:T(8,128)(2,1)} async-done(((bf16[2,2,8,64,512]{4,3,1,0,2:T(8,128)(2,1)}), bf16[2,2,8,64,512]{4,3,1,0,2:T(8,128)(2,1)}, u32[]{:S(2)}, u32[]{:S(2)}) %all-to-all-start) | async-done | bytes 2097184 | tf_op jit(solution)/shard_map/all_to_all | solution.py:55
  134.8 1.8 copy.25
  136.6 3.3 %conditional.13 = (bf16[2,2,512,512]{3,2,1,0:T(8,128)(2,1)S(1)}) conditional(s32[]{:T(128)} %bitcast.37, (bf16[2,2,512,512]{3,2,1,0:T(8,128)(2,1)S(1)}, bf16[2,2,512,512]{3,2,1,0:T(8,128)(2,1)S(1)}) %tuple.78, (bf16[2,2,512,512]{3,2,1,0:T(8,128)(2,1)S(1)}, bf16[2,2,512,512]{3,2,1,0:T(8,128)(2,1)S(1)}) %tuple.79), branch_computations={%region_4.0_spmd, %region_5.0_spmd} | conditional | flops 2150629376 | bytes 23068680
  140.1 51.8 %all_to_all.35 = bf16[2,2,8,64,512]{4,3,1,0,2:T(8,128)(2,1)S(1)} all-to-all(bf16[2,2,8,64,512]{4,3,1,0,2:T(8,128)(2,1)S(1)} %copy.34), channel_id=1, replica_groups=mesh['cuts'=2,'mode'=8,'branch'=2] {'mode'}, dimensions={2} | all-to-all | bytes 4194304 | tf_op jit(solution)/shard_map/all_to_all | solution.py:74
  192.9 1.7 slice_bitcast_fusion.9
  194.8 1.6 collective-permute-done
  196.5 2.0 broadcast_select_fusion.3
  (40 shorter events, 17.6 us)
Async XLA Ops:
  0.0 5.7 %copy-start.6 = (s32[7]{0:T(128)S(1)}, s32[7]{0:T(128)}, u32[]{:S(2)}) copy-start(s32[7]{0:T(128)} %param.11) | copy-start | bytes 88
  7.0 2.4 %copy-start.2 = (bf16[2,2,512,512]{3,2,1,0:T(8,128)(2,1)S(1)}, bf16[2,2,512,512]{3,2,1,0:T(8,128)(2,1)}, u32[]{:S(2)}) copy-start(bf16[2,2,512,512]{3,2,1,0:T(8,128)(2,1)} %get-tuple-element.136) | copy-start | bytes 6291460 | tf_op jit(solution)/shard_map/cond
  7.0 2.8 %copy-start.4 = (bf16[2,2,512,512]{3,2,1,0:T(8,128)(2,1)S(1)}, bf16[2,2,512,512]{3,2,1,0:T(8,128)(2,1)}, u32[]{:S(2)}) copy-start(bf16[2,2,512,512]{3,2,1,0:T(8,128)(2,1)} %get-tuple-element.135) | copy-start | bytes 6291460 | tf_op jit(solution)/shard_map/cond
  26.9 55.7 %all-to-all-start.1 = ((bf16[8,2,2,1,64,512]{5,4,2,1,3,0:T(8,128)(2,1)}), bf16[8,2,2,1,64,512]{5,4,2,1,3,0:T(8,128)(2,1)}, u32[]{:S(2)}, u32[]{:S(2)}) async-start(bf16[8,2,2,1,64,512]{5,4,2,1,3,0:T(8,128)(2,1)} %fusion.116), calls=%async_computation.1 | async-start | bytes 4194304 | tf_op jit(solution)/shard_map/all_to_all | solution.py:59
  34.9 2.1 %copy-start.1 = (bf16[2,2,512,512]{3,2,1,0:T(8,128)(2,1)S(1)}, bf16[2,2,512,512]{3,2,1,0:T(8,128)(2,1)}, u32[]{:S(2)}) copy-start(bf16[2,2,512,512]{3,2,1,0:T(8,128)(2,1)} %get-tuple-element.134) | copy-start | bytes 6291460 | tf_op jit(solution)/shard_map/conditional
  82.6 52.2 %all-to-all-start = ((bf16[2,2,8,64,512]{4,3,1,0,2:T(8,128)(2,1)}), bf16[2,2,8,64,512]{4,3,1,0,2:T(8,128)(2,1)}, u32[]{:S(2)}, u32[]{:S(2)}) async-start(bf16[2,2,8,64,512]{4,3,1,0,2:T(8,128)(2,1)} %copy.24), calls=%async_computation | async-start | bytes 4194304 | tf_op jit(solution)/shard_map/all_to_all | solution.py:55
  191.9 1.0 copy-start.7
  192.1 4.4 %collective-permute-start = (bf16[2,2,512,512]{3,2,1,0:T(8,128)(2,1)S(1)}, bf16[2,2,512,512]{3,2,1,0:T(8,128)(2,1)}, u32[]{:S(2)}, u32[]{:S(2)}) collective-permute-start(bf16[2,2,512,512]{3,2,1,0:T(8,128)(2,1)S(1)} %bitcast.254), channel_id=1, source_target_pairs={{0,1},{1,0},{2,3},{3,2},{4,5},{5,4},{6,7},{7,6},{8,9},{9,8},{10,11... | collective-permute-start | bytes 6291464 | tf_op jit(solution)/shard_map/ppermute | solution.py:10
